TPU v7x, 1024 devices: a whole 8x8x8 slice. The times are simulated.
1024 devices in a mesh: vir: 128 (over x, z_lo, y), ph: 4 (over z_hi), vec: 2 (over core).
Axes of the slice: x: 8, y: 8, z: 8 (z_hi: 4, z_lo: 2; z = z_hi * 2 + z_lo), core: 2. Of those that a mesh axis runs over, the one named last changes fastest.
Arguments:
- vv_factor: bfloat16 [1024, 1024, 1024], P(('ph', 'vec'), 'vir'), may hold values from -0.1875 to 0.1875
- ladder_amp: bfloat16 [1024, 1024, 256], P(None, 'vir'), may hold values from -0.1875 to 0.1875
- cycle_amp: bfloat16 [1024, 32, 128], P(('vir', 'ph'), None, 'vec'), may hold values from -0.015625 to 0.015625
- ov_slots: bfloat16 [2048, 1024, 128], P(('vir', 'ph'), None, 'vec'), may hold values from -6 to 6
- owner_of: int32 [1024], P(('vir', 'ph')), may hold values from 0 to 3, as said below
- slot_of: int32 [1024], P(('vir', 'ph')), may hold values from 0 to 3, as said below
- ov_pairs: bfloat16 [1024, 8, 1024], P(('ph', 'vec'), None, 'vir'), may hold values from -0.1875 to 0.1875
- eps_vir: float32 [1024], replicated, may hold values from 0.5 to 3
- eps_occ: float32 [128], replicated, may hold values from -3 to -0.5
Outputs:
- residual: bfloat16 [1024, 256], P('vir', ('ph', 'vec'))
- update: float32 [1024, 256], P('vir', ('ph', 'vec'))
Inputs may be any that keep to these rules, and one draw needn't show every extreme that they name: `owner_of`: within each run of 8 consecutive blocks (one vir index) one owner holds exactly 4 blocks and no owner more. `slot_of`: distinct among the blocks of one run with the same owner.
All inputs are finite; a program needn't handle non-finite values.
Results may differ from a plain program's by a relative error of at most 0.0055.
Values may be sent and summed in bfloat16 or wider, within the bound.
A program may use at most 64 MiB of HBM per device.

v0:
```python
import jax
import jax.numpy as jnp
from jax import lax
from jax.sharding import Mesh
from jax.sharding import PartitionSpec as P

VIR = ("vir_0", "vir_1", "vir_2")
VIR_PH = ("vir_0", "vir_1", "vir_2", "ph")


def joined_along(pieces, dim):
    pieces = jnp.moveaxis(pieces, 0, dim)
    lengths = pieces.shape
    return pieces.reshape(*lengths[:dim], lengths[dim] * lengths[dim + 1], *lengths[dim + 2 :])


def stacked_from(value, axes, turns):
    pieces = value[None]
    for k in turns:
        pieces = lax.all_gather(pieces, axes[k], axis=0, tiled=True)
    carried = [lax.axis_size(axes[k]) for k in reversed(turns)]
    pieces = pieces.reshape(*carried, *value.shape)
    turned = sorted(range(len(turns)), key=lambda place: turns[len(turns) - 1 - place])
    return pieces.transpose(*turned, *range(len(turns), pieces.ndim)).reshape(-1, *value.shape)


def gather_axes(value, axes, turns, dim):
    return joined_along(stacked_from(value, axes, turns), dim)


def in_blocks(value, dim, devices):
    lengths = value.shape
    pieces = value.reshape(*lengths[:dim], devices, lengths[dim] // devices, *lengths[dim + 1 :])
    return jnp.moveaxis(pieces, dim, 0)


def summed_on_arrival(value, axis, dim):
    devices = lax.axis_size(axis)
    pieces = lax.all_to_all(in_blocks(value, dim, devices), axis, 0, 0, tiled=True)
    return jnp.sum(pieces, axis=0)


def over_axes(value, axes):
    for axis in axes:
        value = lax.psum(value, axis)
    return value


def reduced_to_own(pieces, axes, turns):
    lengths = [lax.axis_size(a) for a in axes]
    pieces = pieces.reshape(*lengths, *pieces.shape[1:])
    pieces = pieces.transpose(*turns, *range(len(axes), pieces.ndim))
    pieces = pieces.reshape(-1, *pieces.shape[len(axes) :])
    for k in turns:
        pieces = lax.psum_scatter(pieces, axes[k], scatter_dimension=0, tiled=True)
    return pieces[0]


def summed_rows(value, axes, turns, dim):
    devices = lax.axis_size(axes)
    return reduced_to_own(in_blocks(value, dim, devices), axes, turns)


def local(
    vv_factor, ladder_amp, cycle_amp, ov_slots, owner_of, slot_of, ov_pairs, eps_vir, eps_occ
):
    chol_local, slab_width, virtuals = vv_factor.shape
    pair_count = ladder_amp.shape[2]
    row_piece = vv_factor[:, :, 0]
    factor_row = gather_axes(row_piece, VIR, (1, 0, 2), 1)
    half = jnp.dot(
        factor_row,
        ladder_amp.reshape(virtuals, slab_width * pair_count),
        preferred_element_type=jnp.float32,
    )
    half = half.astype(jnp.bfloat16).reshape(chol_local * slab_width, pair_count)
    flat_factor = vv_factor.reshape(chol_local * slab_width, virtuals)
    block_local, occ_rows, block_part = cycle_amp.shape
    owner_total = lax.axis_size("ph")
    targets = owner_of[None, :] == jnp.arange(owner_total, dtype=jnp.int32)[:, None]
    outgoing = jnp.where(targets[:, :, None, None], cycle_amp[None], jnp.zeros((), jnp.bfloat16))
    places = jnp.where(targets, slot_of[None, :], 0)
    arrived, arrived_slots = (
        lax.all_to_all(outgoing, "ph", split_axis=0, concat_axis=0, tiled=True),
        lax.all_to_all(places, "ph", split_axis=0, concat_axis=0, tiled=True),
    )
    capacity = ov_slots.shape[0]
    picks = (
        arrived_slots.reshape(-1)[:, None] == jnp.arange(capacity, dtype=jnp.int32)[None, :]
    ).astype(jnp.bfloat16)
    arranged = jnp.einsum(
        "ns,niw->siw",
        picks,
        arrived.reshape(-1, occ_rows, block_part),
        preferred_element_type=jnp.float32,
    )
    arranged = arranged.astype(jnp.bfloat16)
    cycle_part = jnp.einsum("siw,spw->ip", arranged, ov_slots, preferred_element_type=jnp.float32)
    scattered = summed_on_arrival(cycle_part, ("ph", "vec"), 1)
    own_share = over_axes(scattered, VIR)
    coupling = own_share.astype(jnp.bfloat16)
    second_count = ov_pairs.shape[1]
    cycle_term = jnp.einsum("ip,pjb->bij", coupling, ov_pairs, preferred_element_type=jnp.float32)
    cycle_term = cycle_term.reshape(slab_width, occ_rows * second_count)
    slab_start = lax.axis_index(VIR) * slab_width
    full_rows = lax.dot_general(
        flat_factor, half, (((0,), (0,)), ((), ())), preferred_element_type=jnp.float32
    )
    own_rows = lax.dynamic_slice_in_dim(full_rows, slab_start, slab_width, 0)
    paired = summed_on_arrival(
        lax.dynamic_update_slice_in_dim(full_rows, own_rows + cycle_term, slab_start, 0),
        ("ph", "vec"),
        1,
    )
    result = summed_rows(paired, VIR, (0, 2, 1), 0)
    residual = result.astype(jnp.bfloat16)
    share_width = result.shape[1]
    pair_index = lax.axis_index(("ph", "vec")) * share_width + jnp.arange(
        share_width, dtype=jnp.int32
    )
    occ_count = eps_occ.shape[0]
    occ_ids = jnp.arange(occ_count, dtype=jnp.int32)[None, :]
    first_occ = jnp.sum(
        jnp.where((pair_index // second_count)[:, None] == occ_ids, eps_occ[None, :], 0.0), 1
    )
    second_occ = jnp.sum(
        jnp.where((pair_index % second_count)[:, None] == occ_ids, eps_occ[None, :], 0.0), 1
    )
    slab_energy = lax.dynamic_slice_in_dim(eps_vir, slab_start, slab_width, 0)
    denominator = (eps_vir[0] + slab_energy)[:, None] - first_occ[None, :] - second_occ[None, :]
    update = residual.astype(jnp.float32) / denominator
    return (residual, update)


def solution(mesh):
    torus = Mesh(
        mesh.devices.reshape(8, 2, 8, mesh.shape["ph"], mesh.shape["vec"]),
        ("vir_0", "vir_1", "vir_2", "ph", "vec"),
    )
    placed = (
        P(("ph", "vec"), VIR, None),
        P(None, VIR, None),
        P(VIR_PH, None, "vec"),
        P(VIR_PH, None, "vec"),
        P(VIR_PH),
        P(VIR_PH),
        P(("ph", "vec"), None, VIR),
        P(),
        P(),
    )
    return jax.shard_map(
        local,
        mesh=torus,
        in_specs=placed,
        out_specs=(P(VIR, ("ph", "vec")), P(VIR, ("ph", "vec"))),
        check_vma=False,
    )
```

profile of v0, /device:TPU:1, one launch (start us, length us, event | category | flops | bytes accessed | tf_op | source)
XLA Modules:
  0.0 306.1 jit_solution(1951762011536244104)
XLA Ops:
  7.2 0.0 copy-start
  7.2 1.3 compare_select_fusion
  8.5 16.3 %all-to-all-start = ((s32[4,1,2]{2,1,0:T(1,128)}), s32[4,1,2]{2,1,0:T(1,128)S(1)}, u32[]{:S(2)}, u32[]{:S(2)}) async-start(s32[4,1,2]{2,1,0:T(1,128)} %compare_select_fusion), calls=%async_computation | async-start | bytes 4096 | tf_op jit(solution)/shard_map/all_to_all | solution.py:85
  24.8 0.7 iota_compare_fusion.2
  25.4 5.7 %copy.49 = bf16[128,8,8,256]{3,1,2,0:T(8,128)(2,1)} copy(bf16[128,8,8,256]{3,2,1,0:T(8,128)(2,1)} %bitcast.63) | data formatting | bytes 8388608
  31.1 0.2 copy.47
  31.3 3.8 %all-gather = bf16[256,8,1]{0,1,2:T(8,128)(2,1)S(1)} all-gather(bf16[128,8,1]{0,1,2:T(8,128)(2,1)S(1)} %copy.47), channel_id=2, replica_groups=mesh['vir_0'=8,'vir_1'=2,'vir_2'=8,'ph'=4,'vec'=2] {'vir_1'}, dimensions={0}, use_global_device_ids=true | all-gather | bytes 6144 | tf_op jit(solution)/shard_map/all_gather | solution.py:20
  35.1 19.4 %all_gather.10 = bf16[16,128,8]{1,2,0:T(8,128)(2,1)S(1)} all-gather(bf16[2,128,8]{1,2,0:T(8,128)(2,1)S(1)} %bitcast.70), channel_id=1, replica_groups=mesh['vir_0'=8,'vir_1'=2,'vir_2'=8,'ph'=4,'vec'=2] {'vir_0'}, dimensions={0}, use_global_device_ids=true | all-gather | bytes 36864 | tf_op jit(solution)/shard_map/all_gather | solution.py:20
  54.5 20.7 %all_gather.11 = bf16[128,128,8]{1,2,0:T(8,128)(2,1)S(1)} all-gather(bf16[16,128,8]{1,2,0:T(8,128)(2,1)S(1)} %all_gather.10), channel_id=1, replica_groups=mesh['vir_0'=8,'vir_1'=2,'vir_2'=8,'ph'=4,'vec'=2] {'vir_2'}, dimensions={0}, use_global_device_ids=true | all-gather | bytes 294912 | tf_op jit(solution)/shard_map/all_gather | solution.py:20
  75.2 0.1 copy.39
  75.3 0.1 fusion.10
  75.4 0.7 reshape.169
  76.1 6.7 %all-to-all-start.1 = ((bf16[4,2,2048]{2,1,0:T(2,128)(2,1)}), bf16[4,2,2048]{2,1,0:T(2,128)(2,1)S(1)}, u32[]{:S(2)}, u32[]{:S(2)}) async-start(bf16[4,2,2048]{2,1,0:T(2,128)(2,1)} %reshape.169), calls=%async_computation.1 | async-start | bytes 65536 | tf_op jit(solution)/shard_map/all_to_all | solution.py:84
  82.8 2.9 convolution_convert_fusion
  85.8 0.2 reshape.147
  86.0 0.5 broadcast.132
  86.5 0.7 reduce.3
  87.2 0.1 eq.76
  87.3 2.2 all-to-all-done.1
  89.5 0.1 reshape.170
  89.7 0.1 convolution_convert_fusion.1
  89.8 0.2 convolution_bitcast_fusion
  90.1 0.7 copy.53
  90.7 20.1 %all-to-all-start.2 = ((f32[8,32,128]{2,1,0:T(8,128)}), f32[8,32,128]{2,1,0:T(8,128)S(1)}, u32[]{:S(2)}, u32[]{:S(2)}) async-start(f32[8,32,128]{2,1,0:T(8,128)} %bitcast.59), calls=%async_computation.2 | async-start | bytes 262144 | tf_op jit(solution)/shard_map/all_to_all | solution.py:39
  110.8 2.3 fusion
  113.1 6.4 %all-to-all-done.2 = f32[8,32,128]{2,1,0:T(8,128)S(1)} async-done(((f32[8,32,128]{2,1,0:T(8,128)}), f32[8,32,128]{2,1,0:T(8,128)S(1)}, u32[]{:S(2)}, u32[]{:S(2)}) %all-to-all-start.2) | async-done | bytes 131104 | tf_op jit(solution)/shard_map/all_to_all | solution.py:39
  119.5 21.4 %psum.21 = f32[32,128]{1,0:T(8,128)S(1)} all-reduce(f32[32,128]{1,0:T(8,128)S(1)} %reduce_sum.36), channel_id=1, replica_groups=mesh['vir_0'=8,'vir_1'=2,'vir_2'=8,'ph'=4,'vec'=2] {'vir_0'}, use_global_device_ids=true, to_apply=%region_1.2 | all-reduce | flops 4096 | bytes 32768 | tf_op jit(solution)/shard_map/psum | solution.py:45
  140.9 6.5 %psum.22 = f32[32,128]{1,0:T(8,128)S(1)} all-reduce(f32[32,128]{1,0:T(8,128)S(1)} %psum.21), channel_id=1, replica_groups=mesh['vir_0'=8,'vir_1'=2,'vir_2'=8,'ph'=4,'vec'=2] {'vir_1'}, use_global_device_ids=true, to_apply=%region_2.3 | all-reduce | flops 4096 | bytes 32768 | tf_op jit(solution)/shard_map/psum | solution.py:45
  147.5 21.6 %psum.23 = bf16[32,128]{1,0:T(8,128)(2,1)S(1)} all-reduce(f32[32,128]{1,0:T(8,128)S(1)} %psum.22), channel_id=1, replica_groups=mesh['vir_0'=8,'vir_1'=2,'vir_2'=8,'ph'=4,'vec'=2] {'vir_2'}, use_global_device_ids=true, to_apply=%region_3.4 | all-reduce | flops 4096 | bytes 24576 | tf_op jit(solution)/shard_map/psum | solution.py:45
  169.1 0.1 convolution_bitcast_fusion.1
  169.2 0.1 copy.44
  169.3 0.1 bitcast_add_fusion
  169.5 1.1 dynamic_update_slice.3
  170.5 46.5 %all_to_all.21 = f32[8,1024,32]{1,2,0:T(8,128)S(1)} all-to-all(f32[8,1024,32]{1,2,0:T(8,128)S(1)} %bitcast.62), channel_id=1, replica_groups=mesh['vir_0'=8,'vir_1'=2,'vir_2'=8,'ph'=4,'vec'=2] {'ph','vec'}, dimensions={0} | all-to-all | bytes 2097152 | tf_op jit(solution)/shard_map/all_to_all | solution.py:39
  217.0 0.1 reduce_sum.37
  217.1 0.2 copy.45
  217.3 0.8 copy.46
  218.1 0.0 reduce-scatter.3.cloned.1.call-update
  218.2 0.0 reduce-scatter.5.cloned.1.call-start
  218.2 1.2 slice.7
  219.4 0.2 select_reduce_fusion.1
  219.6 29.1 %reduce-scatter.3.cloned.1.call-done = f32[16,8,32]{2,1,0:T(8,128)} async-done(((f32[128,8,32]{2,1,0:T(8,128)}), f32[16,8,32]{2,1,0:T(8,128)}) %reduce-scatter.3.cloned.1.call-update) | async-done | bytes 16400 | tf_op jit(solution)/shard_map/reduce_scatter | solution.py:55
  248.7 0.0 reduce-scatter.5.cloned.1.call-update
  248.7 1.4 dynamic-slice_add_fusion
  250.1 1.3 dynamic-slice.4
  251.4 42.1 %reduce-scatter.5.cloned.1.call-done = f32[2,8,32]{2,1,0:T(8,128)} async-done(((f32[16,8,32]{2,1,0:T(8,128)}), f32[2,8,32]{2,1,0:T(8,128)}) %reduce-scatter.5.cloned.1.call-update) | async-done | bytes 2064 | tf_op jit(solution)/shard_map/reduce_scatter | solution.py:55
  293.5 4.5 %all-reduce = bf16[2,8,32]{2,1,0:T(8,128)(2,1)S(1)} all-reduce(f32[2,8,32]{2,1,0:T(8,128)} %reduce-scatter.5.cloned.1.call-done), channel_id=5, replica_groups=mesh['vir_0'=8,'vir_1'=2,'vir_2'=8,'ph'=4,'vec'=2] {'vir_1'}, use_global_device_ids=true, to_apply=%region_7.8.clone | all-reduce | flops 512 | bytes 3072
  298.0 1.2 subtract_divide_fusion
  (15 shorter events, 0.1 us)
Async XLA Ops:
  7.2 82.7 %copy-start = (bf16[4,1024,64]{1,2,0:T(8,128)(2,1)S(1)}, bf16[4,1024,64]{1,2,0:T(8,128)(2,1)}, u32[]{:S(2)}) copy-start(bf16[4,1024,64]{1,2,0:T(8,128)(2,1)} %param.12) | copy-start | bytes 1572868
  8.5 67.6 %all-to-all-start = ((s32[4,1,2]{2,1,0:T(1,128)}), s32[4,1,2]{2,1,0:T(1,128)S(1)}, u32[]{:S(2)}, u32[]{:S(2)}) async-start(s32[4,1,2]{2,1,0:T(1,128)} %compare_select_fusion), calls=%async_computation | async-start | bytes 4096 | tf_op jit(solution)/shard_map/all_to_all | solution.py:85
  25.4 5.7 %slice-start = ((bf16[128,8,1024]{2,1,0:T(8,128)(2,1)}), bf16[128,8,1]{2,1,0:T(8,128)(2,1)S(1)}, s32[]{:S(2)}) async-start(bf16[128,8,1024]{2,1,0:T(8,128)(2,1)} %param.9), calls=%async_computation.8 | async-start | bytes 524288 | tf_op jit(solution)/shard_map/slice | solution.py:69
  25.4 49.8 %copy-start.2 = (bf16[2,32,64]{2,1,0:T(8,128)(2,1)S(1)}, bf16[2,32,64]{2,1,0:T(8,128)(2,1)}, u32[]{:S(2)}) copy-start(bf16[2,32,64]{2,1,0:T(8,128)(2,1)} %param.11) | copy-start | bytes 24580
  76.1 13.4 %all-to-all-start.1 = ((bf16[4,2,2048]{2,1,0:T(2,128)(2,1)}), bf16[4,2,2048]{2,1,0:T(2,128)(2,1)S(1)}, u32[]{:S(2)}, u32[]{:S(2)}) async-start(bf16[4,2,2048]{2,1,0:T(2,128)(2,1)} %reshape.169), calls=%async_computation.1 | async-start | bytes 65536 | tf_op jit(solution)/shard_map/all_to_all | solution.py:84
  85.7 83.3 %copy-start.1 = (bf16[128,8,8]{0,2,1:T(8,128)(2,1)S(1)}, bf16[128,8,8]{0,2,1:T(8,128)(2,1)}, u32[]{:S(2)}) copy-start(bf16[128,8,8]{0,2,1:T(8,128)(2,1)} %param.15) | copy-start | bytes 49156
  90.7 28.8 %all-to-all-start.2 = ((f32[8,32,128]{2,1,0:T(8,128)}), f32[8,32,128]{2,1,0:T(8,128)S(1)}, u32[]{:S(2)}, u32[]{:S(2)}) async-start(f32[8,32,128]{2,1,0:T(8,128)} %bitcast.59), calls=%async_computation.2 | async-start | bytes 262144 | tf_op jit(solution)/shard_map/all_to_all | solution.py:39
  110.8 137.9 %reduce-scatter.3.cloned.1.call-start = ((), (), s32[]{:S(2)}) async-start(), calls=%async_computation.6 | async-start | bytes 589824 | tf_op jit(solution)/shard_map/reduce_scatter | solution.py:55
  113.1 106.3 %copy-start.3 = (f32[128]{0:T(128)S(1)}, f32[128]{0:T(128)}, u32[]{:S(2)}) copy-start(f32[128]{0:T(128)} %param.17) | copy-start | bytes 1540
  218.2 75.3 %reduce-scatter.5.cloned.1.call-start = ((), (), s32[]{:S(2)}) async-start(), calls=%async_computation.7 | async-start | bytes 73728 | tf_op jit(solution)/shard_map/reduce_scatter | solution.py:55
Sparse Core Ops, SparseCore 0:
  218.3 30.3 reduce-scatter.2
  252.1 41.3 reduce-scatter.4
where the time goes:
time: 312 us; the launch traced here: 306 us
  blocking collectives  144 us (46%)
  waiting for transfers between devices  79.8 us (26%)
  starting transfers between devices  43.1 us (14%)
  between operations  14.2 us (5%)
  local copies, waits for them, and re-layouts  13 us (4%)
  other arithmetic  5.76 us (2%)
  matrix products  5.73 us (2%)
    reduce_scatter x2, waiting for transfers between devices, reduced_to_own(): pieces = lax.psum_scatter(pieces, axes[k], scatter_dimension=0, tiled=True)  71.2 us
    psum x3, blocking collectives, over_axes(): value = lax.psum(value, axis)  49.6 us
    all_to_all x1, blocking collectives, summed_on_arrival(): lax.all_to_all(in_blocks(value, dim, devices), axis, 0, 0, tiled=True)  46.5 us
    all_gather x3, blocking collectives, stacked_from(): pieces = lax.all_gather(pieces, axes[k], axis=0, tiled=True)  43.9 us
    all_to_all x1, starting transfers between devices, summed_on_arrival(): lax.all_to_all(in_blocks(value, dim, devices), axis, 0, 0, tiled=True)  20.1 us
    all_to_all x1, starting transfers between devices, local(): lax.all_to_all(places, 'ph', split_axis=0, concat_axis=0, tiled=True)  16.3 us
    unnamed x14, local copies, waits for them, and re-layouts  7.99 us
    all_to_all x1, starting transfers between devices, local(): lax.all_to_all(outgoing, 'ph', split_axis=0, concat_axis=0, tiled=True)  6.69 us
  transfers between devices with their start and end apart: 5, of which 4 were waited for; matrix products, arithmetic and copies ran while one was open for 6% of the time, Pallas kernels for 0%

commit v1 on v0

v1 whole, which is shorter than its diff:
```python
import functools

import jax
import jax.numpy as jnp
from jax import lax
from jax.experimental import pallas as pl
from jax.experimental.pallas import tpu as pltpu
from jax.sharding import Mesh
from jax.sharding import PartitionSpec as P

AXES = ("vir_0", "vir_1", "vir_2", "ph", "vec")
VIR = ("vir_0", "vir_1", "vir_2")
VIR_PH = ("vir_0", "vir_1", "vir_2", "ph")
F32 = jnp.float32
BF16 = jnp.bfloat16
R = 8
LANES = 128


def far_first(count):
    return sorted(range(1, count), key=lambda d: -min(d, count - d))


def body(
    sizes,
    factor,
    amp,
    cycle_amp,
    ov_slots,
    owner_of,
    slot_of,
    ov_pairs,
    eps_vir,
    eps_occ,
    residual_ref,
    update_ref,
    factor_raw,
    factor_wide,
    factor_t,
    amp_raw,
    amp_wide,
    amp_d,
    rows,
    row_lhs,
    half,
    slots_v,
    cyc_v,
    pairs_v,
    blk_send,
    blk_recv,
    part,
    part_recv,
    c1,
    c1_recv,
    c2,
    c2_recv,
    c3,
    c3_recv,
    cyc,
    cyc_recv,
    grid,
    grid_recv,
    wide,
    stage,
    stage_recv,
    second,
    second_recv,
    third,
    third_recv,
    load_sem,
    send_sem,
    recv_sem,
):
    nx, nl, ny, nh, nk = sizes
    pc = factor.shape[0]
    pairs = amp.shape[2]
    slab = nl * ny * R
    part_rows = ny * R
    x, l, y, h, k = (lax.axis_index(a) for a in AXES)
    me = {"vir_0": x, "vir_1": l, "vir_2": y, "ph": h, "vec": k}

    def at(**moved):
        return tuple(moved.get(a, me[a]) for a in AXES)

    def step(axis, value, d, count):
        return {axis: lax.rem(value + d, count)}

    ids = iter(range(1000))

    def remote(src, dst, target, slot):
        return pltpu.make_async_remote_copy(
            src_ref=src,
            dst_ref=dst,
            send_sem=send_sem.at[slot],
            recv_sem=recv_sem.at[slot],
            device_id=target,
            device_id_type=pl.DeviceIdType.MESH,
        )

    sent = []

    def start(copies):
        for c in copies:
            c.start()
        sent.extend(copies)

    def arrive(copies):
        for c in copies:
            c.wait_recv()

    x_steps, y_steps = far_first(nx), far_first(ny)
    z_steps = [(dh, dk) for dh in range(nh) for dk in range(nk) if dh or dk]

    barrier = pltpu.get_barrier_semaphore()
    partners = [step("vir_0", x, d, nx) for d in x_steps]
    partners += [step("vir_2", y, d, ny) for d in y_steps]
    partners += [
        {**step("ph", h, dh, nh), **step("vec", k, dk, nk), **step("vir_1", l, dl, nl)}
        for dl in range(nl)
        for dh in range(nh)
        for dk in range(nk)
        if dl or dh or dk
    ]
    for moved in partners:
        pl.semaphore_signal(
            barrier, inc=1, device_id=at(**moved), device_id_type=pl.DeviceIdType.MESH
        )

    loads = []

    def load(src, dst):
        copy = pltpu.make_async_copy(src, dst, load_sem.at[len(loads)])
        copy.start()
        loads.append(copy)
        return copy

    factor_loads = [
        load(factor.at[:, :, pl.ds(s * slab, slab)], factor_raw.at[s]) for s in range(nx)
    ]
    cyc_load = load(cycle_amp, cyc_v)
    slots_load = load(ov_slots, slots_v)
    amp_loads = [
        load(amp.at[pl.ds(s * slab, slab)], amp_raw.at[pl.ds(s * slab, slab)]) for s in range(nx)
    ]
    pairs_load = load(ov_pairs, pairs_v)

    cyc_load.wait()
    blocks = [jnp.concatenate([cyc_v[n].astype(F32)] * 2, axis=1) for n in range(2)]
    lane_half = (
        lax.broadcasted_iota(jnp.int32, blocks[0].shape, 1) >= blocks[0].shape[1] // 2
    ).astype(jnp.int32)
    for target in range(nh):
        for pair in range(2):
            total = jnp.zeros_like(blocks[0])
            for n in range(2):
                wanted = jnp.where(owner_of[n] == target, slot_of[n], -1)
                total = total + jnp.where(lane_half + 2 * pair == wanted, blocks[n], 0.0)
            blk_send[target, pair] = total.astype(BF16)

    factor_loads[0].wait()
    first = factor_raw[0].astype(F32)[:, :, :1]
    lane_of = lax.broadcasted_iota(jnp.int32, (pc, R, pc), 2)
    row_of = lax.broadcasted_iota(jnp.int32, (pc, R, pc), 0)
    piece = jnp.sum(jnp.where(lane_of == row_of, first, 0.0), axis=0).astype(BF16)
    outer = jnp.where(l == 0, y, x)
    inner = jnp.where(l == 0, x, y)
    rows[l, outer, inner] = piece

    pl.semaphore_wait(barrier, len(partners))

    pick = rows.at[l, outer, inner]
    gather0 = [remote(pick, pick, at(**step("vir_1", l, 1, nl)), next(ids))]
    start(gather0)
    to_owner = []
    for d in far_first(nh):
        moved = step("ph", h, d, nh)
        to_owner.append(
            remote(blk_send.at[moved["ph"]], blk_recv.at[d - 1], at(**moved), next(ids))
        )
    start(to_owner)

    arrive(gather0)
    gather1 = []
    for dx, dy in zip(x_steps, y_steps):
        own0, own1 = rows.at[0, y, x], rows.at[1, x, y]
        gather1.append(remote(own0, own0, at(**step("vir_0", x, dx, nx)), next(ids)))
        gather1.append(remote(own1, own1, at(**step("vir_2", y, dy, ny)), next(ids)))
    start(gather1)

    for copy in factor_loads[1:]:
        copy.wait()

    def turn_factor(s, carry):
        factor_wide[...] = factor_raw[s].astype(F32).reshape(factor_wide.shape)
        base = pl.multiple_of(s * part_rows, part_rows)
        for d in range(R):
            turned = factor_wide[pl.ds(d, pc, stride=R), :].T.astype(BF16)
            for c in range(nl):
                factor_t[c, pl.ds(base, part_rows), d * pc : (d + 1) * pc] = turned[
                    c * part_rows : (c + 1) * part_rows
                ]
        return carry

    lax.fori_loop(0, nx, turn_factor, 0)

    slots_load.wait()
    arrive(to_owner)
    arranged = blk_send[h].astype(F32)
    for d in range(nh - 1):
        arranged = arranged + blk_recv[d].astype(F32)
    arranged = arranged.astype(BF16)
    depth = slots_v.shape[0] // 2
    for q in range(nh * nk):
        chunk = slice(q * pc, (q + 1) * pc)
        part[q] = jnp.dot(
            arranged[0], slots_v[:depth, chunk], preferred_element_type=F32
        ) + jnp.dot(arranged[1], slots_v[depth:, chunk], preferred_element_type=F32)
    to_chunk = []
    for n, (dh, dk) in enumerate(z_steps):
        moved = {**step("ph", h, dh, nh), **step("vec", k, dk, nk)}
        to_chunk.append(
            remote(
                part.at[moved["ph"] * nk + moved["vec"]], part_recv.at[n], at(**moved), next(ids)
            )
        )
    start(to_chunk)

    arrive(gather1)
    gather2 = []
    for dx, dy in zip(x_steps, y_steps):
        own0, own1 = rows.at[0, y], rows.at[1, x]
        gather2.append(remote(own0, own0, at(**step("vir_2", y, dy, ny)), next(ids)))
        gather2.append(remote(own1, own1, at(**step("vir_0", x, dx, nx)), next(ids)))
    start(gather2)

    for copy in amp_loads:
        copy.wait()

    def split_amp(s, carry):
        base = pl.multiple_of(s * slab, slab)
        chunk = amp_raw[pl.ds(base, slab)].astype(F32)
        for n in range(pairs // LANES):
            amp_wide[n] = chunk[:, :, n * LANES : (n + 1) * LANES].reshape(slab * R, LANES)
        for d in range(R):
            for n in range(pairs // LANES):
                amp_d[d, pl.ds(base, slab), n * LANES : (n + 1) * LANES] = amp_wide[
                    n, pl.ds(d, slab, stride=R), :
                ].astype(BF16)
        return carry

    lax.fori_loop(0, nx, split_amp, 0)

    arrive(to_chunk)
    total = part[h * nk + k]
    for n in range(len(z_steps)):
        total = total + part_recv[n]
    mid = total.shape[0] // 2
    c1[0], c1[1] = total[:mid], total[mid:]
    sum1 = []
    for dx, dy in zip(x_steps, y_steps):
        sum1.append(
            remote(c1.at[0], c1_recv.at[0, dx - 1], at(**step("vir_0", x, dx, nx)), next(ids))
        )
        sum1.append(
            remote(c1.at[1], c1_recv.at[1, dy - 1], at(**step("vir_2", y, dy, ny)), next(ids))
        )
    start(sum1)

    arrive(gather2)
    for s in range(nx):
        low = rows[0, :, s].astype(F32).reshape(part_rows, pc)
        high = rows[1, s].astype(F32).reshape(part_rows, pc)
        row_lhs[:, s * slab : (s + 1) * slab] = jnp.concatenate([low, high], axis=0).T.astype(BF16)

    def make_half(d, carry):
        half[pl.ds(pl.multiple_of(d * pc, pc), pc), :] = jnp.dot(
            row_lhs[...], amp_d[d], preferred_element_type=F32
        ).astype(BF16)
        return carry

    lax.fori_loop(0, R, make_half, 0)

    swap = []
    for c in range(nl):
        full = jnp.dot(factor_t[c], half[...], preferred_element_type=F32)
        for n in range(nk):
            grid[c, n] = full[:, n * LANES : (n + 1) * LANES].reshape(nx, ny, R, LANES)
        swap.append(
            remote(grid.at[c, 1 - k], grid_recv.at[c], at(**step("vec", k, 1, nk)), next(ids))
        )
        start(swap[-1:])

    scatter1 = []
    for c in range(nl):
        arrive(swap[c : c + 1])
        wide[c] = grid[c, k] + grid_recv[c]
        if c == 0:
            stage[0] = wide[0].astype(BF16)
        else:
            for s in range(nx):
                for t in range(ny):
                    stage[1, t, s] = wide[1, s, t].astype(BF16)
        copies = []
        for d in x_steps if c == 0 else y_steps:
            moved = step("vir_0", x, d, nx) if c == 0 else step("vir_2", y, d, ny)
            there = moved["vir_0"] if c == 0 else moved["vir_2"]
            copies.append(
                remote(stage.at[c, there], stage_recv.at[c, d - 1], at(**moved), next(ids))
            )
        start(copies)
        scatter1.append(copies)

    arrive(sum1)
    for c in range(2):
        total = c1[c]
        for d in range(nx - 1):
            total = total + c1_recv[c, d]
        c2[c] = total
    sum2 = []
    for dx, dy in zip(x_steps, y_steps):
        sum2.append(
            remote(c2.at[0], c2_recv.at[0, dy - 1], at(**step("vir_2", y, dy, ny)), next(ids))
        )
        sum2.append(
            remote(c2.at[1], c2_recv.at[1, dx - 1], at(**step("vir_0", x, dx, nx)), next(ids))
        )
    start(sum2)

    scatter2 = []
    for c in range(nl):
        arrive(scatter1[c])
        total = wide[0, x] if c == 0 else wide[1, :, y]
        for d in range(nx - 1):
            total = total + stage_recv[c, d].astype(F32)
        second[c] = total
        copies = []
        for d in y_steps if c == 0 else x_steps:
            moved = step("vir_2", y, d, ny) if c == 0 else step("vir_0", x, d, nx)
            there = moved["vir_2"] if c == 0 else moved["vir_0"]
            copies.append(
                remote(second.at[c, there], second_recv.at[c, d - 1], at(**moved), next(ids))
            )
        start(copies)
        scatter2.append(copies)

    arrive(sum2)
    for c in range(2):
        total = c2[c]
        for d in range(nx - 1):
            total = total + c2_recv[c, d]
        c3[c * mid : (c + 1) * mid] = total
    sum3 = [remote(c3, c3_recv, at(**step("vir_1", l, 1, nl)), next(ids))]
    start(sum3)
    arrive(sum3)
    coupling = c3[...] + c3_recv[...]
    occ = coupling.shape[0]
    spread = jnp.broadcast_to(coupling[:, None, :], (occ, R, pc)).reshape(occ * R, pc)
    pairs_load.wait()
    second_count = ov_pairs.shape[0]
    ov = pairs_v[...].astype(F32).reshape(second_count * R, pc).astype(BF16)
    every = lax.dot_general(
        ov, spread.astype(BF16), (((1,), (1,)), ((), ())), preferred_element_type=F32
    )
    lane_j = lax.rem(lax.broadcasted_iota(jnp.int32, (R, pairs), 1), second_count)
    term = jnp.zeros((R, pairs), F32)
    for j in range(second_count):
        term = term + jnp.where(lane_j == j, every[j * R : (j + 1) * R], 0.0)
    for n in range(nk):
        cyc[n] = term[:, n * LANES : (n + 1) * LANES]
    swap_cyc = [remote(cyc.at[1 - k], cyc_recv, at(**step("vec", k, 1, nk)), next(ids))]
    start(swap_cyc)

    width = residual_ref.shape[1]
    per_half = LANES // width
    q = h * nk + k
    line = lax.broadcasted_iota(jnp.int32, (R, width), 0)
    lane = lax.broadcasted_iota(jnp.int32, (R, width), 1)
    slab_start = ((x * nl + l) * ny + y) * R
    virtual = jnp.zeros((R, width), F32)
    for r in range(R):
        virtual = jnp.where(line == r, eps_vir[slab_start + r], virtual)
    first_occ = jnp.zeros((R, width), F32)
    for n in range(width // second_count):
        first_occ = jnp.where(
            lane // second_count == n, eps_occ[q * (width // second_count) + n], first_occ
        )
    second_occ = jnp.zeros((R, width), F32)
    for n in range(second_count):
        second_occ = jnp.where(lax.rem(lane, second_count) == n, eps_occ[n], second_occ)
    denominator = (eps_vir[0] + virtual) - first_occ - second_occ

    arrive(swap_cyc)
    cycle_half = cyc[k] + cyc_recv[...]
    for c in range(nl):
        arrive(scatter2[c])
        total = second[0, y] if c == 0 else second[1, x]
        for d in range(nx - 1):
            total = total + second_recv[c, d]
        third[c] = total + jnp.where(l == c, cycle_half, 0.0)

    base_id = next(ids)
    mine = h * nl + l
    finals = []
    for m in range(per_half):
        for c in range(nl):
            there = k * per_half + m
            th, tk = there // nk, lax.rem(there, nk)
            away = jnp.logical_not((th == h) & (tk == k) & (c == l))
            copy = pltpu.make_async_remote_copy(
                src_ref=third.at[c],
                dst_ref=third_recv.at[mine],
                send_sem=send_sem.at[base_id + m * nl + c],
                recv_sem=recv_sem.at[base_id + mine],
                device_id=at(ph=th, vec=tk, vir_1=jnp.int32(c)),
                device_id_type=pl.DeviceIdType.MESH,
            )
            finals.append((away, copy))
            pl.when(away)(copy.start)
    own_source = q // per_half == k

    @pl.when(own_source)
    def _():
        third_recv[mine] = third[l]

    for s in range(nh * nl):
        from_other = jnp.logical_not(own_source & (mine == s))
        copy = pltpu.make_async_remote_copy(
            src_ref=third.at[0],
            dst_ref=third_recv.at[s],
            send_sem=send_sem.at[base_id],
            recv_sem=recv_sem.at[base_id + s],
            device_id=at(**step("vir_1", l, 1, nl)),
            device_id_type=pl.DeviceIdType.MESH,
        )
        pl.when(from_other)(copy.wait_recv)

    total = third_recv[0]
    for s in range(1, nh * nl):
        total = total + third_recv[s]
    mine_lanes = lax.rem(q, per_half)
    result = jnp.zeros((R, width), F32)
    for m in range(per_half):
        result = jnp.where(mine_lanes == m, total[:, m * width : (m + 1) * width], result)
    rounded = result.astype(BF16)
    residual_ref[...] = rounded
    update_ref[...] = rounded.astype(F32) / denominator

    for copy in sent:
        copy.wait_send()
    for away, copy in finals:
        pl.when(away)(copy.wait_send)


def local(
    sizes,
    vv_factor,
    ladder_amp,
    cycle_amp,
    ov_slots,
    owner_of,
    slot_of,
    ov_pairs,
    eps_vir,
    eps_occ,
):
    nx, nl, ny, nh, nk = sizes
    pc, _, virtuals = vv_factor.shape
    pairs = ladder_amp.shape[2]
    capacity, chol, part_w = ov_slots.shape
    occ = cycle_amp.shape[1]
    second_count = ov_pairs.shape[1]
    slots_t = jnp.transpose(ov_slots, (0, 2, 1)).reshape(capacity * part_w, chol)
    pairs_t = jnp.transpose(ov_pairs, (1, 2, 0))
    slab = nl * ny * R
    width = pairs // (nh * nk)
    steps = nx - 1
    VM = pltpu.VMEM
    scratch = [
        VM((nx, pc, R, slab), BF16),
        VM((pc * R, slab), F32),
        VM((nl, nx * ny * R, R * pc), BF16),
        VM(ladder_amp.shape, BF16),
        VM((pairs // LANES, slab * R, LANES), F32),
        VM((R, virtuals, pairs), BF16),
        VM((nl, nx, ny, R, pc), BF16),
        VM((pc, virtuals), BF16),
        VM((R * pc, pairs), BF16),
        VM(slots_t.shape, BF16),
        VM(cycle_amp.shape, BF16),
        VM(pairs_t.shape, BF16),
        VM((nh, 2, occ, 2 * part_w), BF16),
        VM((nh - 1, 2, occ, 2 * part_w), BF16),
        VM((nh * nk, occ, pc), F32),
        VM((nh * nk - 1, occ, pc), F32),
        VM((2, occ // 2, pc), F32),
        VM((2, steps, occ // 2, pc), F32),
        VM((2, occ // 2, pc), F32),
        VM((2, steps, occ // 2, pc), F32),
        VM((occ, pc), F32),
        VM((occ, pc), F32),
        VM((nk, R, LANES), F32),
        VM((R, LANES), F32),
        VM((nl, nk, nx, ny, R, LANES), F32),
        VM((nl, nx, ny, R, LANES), F32),
        VM((nl, nx, ny, R, LANES), F32),
        VM((nl, nx, ny, R, LANES), BF16),
        VM((nl, steps, ny, R, LANES), BF16),
        VM((nl, ny, R, LANES), F32),
        VM((nl, steps, R, LANES), F32),
        VM((nl, R, LANES), F32),
        VM((nh * nl, R, LANES), F32),
        pltpu.SemaphoreType.DMA((2 * nx + 3,)),
        pltpu.SemaphoreType.DMA((128,)),
        pltpu.SemaphoreType.DMA((128,)),
    ]
    hbm = pl.BlockSpec(memory_space=pltpu.MemorySpace.HBM)
    smem = pl.BlockSpec(memory_space=pltpu.SMEM)
    vmem = pl.BlockSpec(memory_space=pltpu.VMEM)
    return pl.pallas_call(
        functools.partial(body, sizes),
        out_shape=(
            jax.ShapeDtypeStruct((R, width), BF16),
            jax.ShapeDtypeStruct((R, width), F32),
        ),
        in_specs=[hbm, hbm, hbm, hbm, smem, smem, hbm, smem, smem],
        out_specs=(vmem, vmem),
        scratch_shapes=scratch,
        compiler_params=pltpu.CompilerParams(
            collective_id=0, has_side_effects=True, vmem_limit_bytes=63 * 1024 * 1024
        ),
    )(
        vv_factor,
        ladder_amp,
        cycle_amp,
        slots_t,
        owner_of,
        slot_of,
        pairs_t,
        eps_vir,
        eps_occ,
    )


def build(devices, sizes):
    torus = Mesh(devices.reshape(sizes), AXES)
    placed = (
        P(("ph", "vec"), VIR, None),
        P(None, VIR, None),
        P(VIR_PH, None, "vec"),
        P(VIR_PH, None, "vec"),
        P(VIR_PH),
        P(VIR_PH),
        P(("ph", "vec"), None, VIR),
        P(),
        P(),
    )
    return jax.shard_map(
        functools.partial(local, sizes),
        mesh=torus,
        in_specs=placed,
        out_specs=(P(VIR, ("ph", "vec")), P(VIR, ("ph", "vec"))),
        check_vma=False,
    )


def solution(mesh):
    return build(mesh.devices, (8, 2, 8, mesh.shape["ph"], mesh.shape["vec"]))
```

time: 312 us -> 62.2 us (0.20); the launches traced: 306 us -> 62 us
  blocking collectives: 144 us -> 0 us
  waiting for transfers between devices: 79.8 us -> 0 us
  Pallas kernels: 0 us -> 58.8 us
  starting transfers between devices: 43.1 us -> 0 us
  between operations: 14.2 us -> 0.64 us
  local copies, waits for them, and re-layouts: 13 us -> 2.5 us
  other arithmetic: 5.76 us -> 0 us
  matrix products: 5.73 us -> 0 us
    reduce_scatter x2 -> x0, waiting for transfers between devices: 71.2 us -> none  [reduced_to_own(): pieces = lax.psum_scatter(pieces, axes[k], scatter_dimension=0, tiled=True)]
    pallas_call x0 -> x1, Pallas kernels: none -> 58.8 us  [local(): pl.pallas_call(functools.partial(body, sizes), out_shape=(jax.ShapeDtypeS...]
    psum x3 -> x0, blocking collectives: 49.6 us -> none  [over_axes(): value = lax.psum(value, axis)]
    all_to_all x1 -> x0, blocking collectives: 46.5 us -> none  [summed_on_arrival(): lax.all_to_all(in_blocks(value, dim, devices), axis, 0, 0, tiled=True)]
    all_gather x3 -> x0, blocking collectives: 43.9 us -> none  [stacked_from(): pieces = lax.all_gather(pieces, axes[k], axis=0, tiled=True)]
    all_to_all x3 -> x0, starting transfers between devices: 43 us -> none  [the longest x1 20.1 us: summed_on_arrival(): lax.all_to_all(in_blocks(value, dim, devices), axis, 0, 0, tiled=True)]
    all_to_all x3 -> x0, waiting for transfers between devices: 8.61 us -> none  [the longest x1 6.37 us: summed_on_arrival(): lax.all_to_all(in_blocks(value, dim, devices), axis, 0, 0, tiled=True)]
    dot_general x4 -> x0, matrix products: 5.61 us -> none  [the longest x1 2.93 us: local(): jnp.dot(factor_row, ladder_amp.reshape(virtuals, slab_width * pair_count)...]
  transfers between devices with their start and end apart: 5 -> 0, of which waited for: 4 -> 0; matrix products, arithmetic and copies ran while one was open for 6% -> 0% of each run, Pallas kernels for 0% -> 0%
where the time goes in v1:
time: 62.2 us; the launch traced here: 62 us
  Pallas kernels  58.8 us (95%)
  local copies, waits for them, and re-layouts  2.5 us (4%)
  between operations  0.64 us (1%)
    pallas_call x1, Pallas kernels, local(): pl.pallas_call(functools.partial(body, sizes), out_shape=(jax.ShapeDtypeS...  58.8 us
    unnamed x2, local copies, waits for them, and re-layouts  2.5 us

profile of v1, /device:TPU:1, one launch (start us, length us, event | category | flops | bytes accessed | tf_op | source)
XLA Modules:
  0.0 62.0 jit_solution(16218685518212272591)
XLA Ops:
  0.6 58.8 %shard_map.104 = (bf16[8,32]{1,0:T(8,128)(2,1)}, f32[8,32]{1,0:T(8,128)}) custom-call(bf16[128,8,1024]{2,1,0:T(8,128)(2,1)} %factor.1, bf16[1024,8,256]{2,1,0:T(8,128)(2,1)} %amp.1, bf16[2,32,64]{2,1,0:T(8,128)(2,1)} %cycle_amp.1, bf16[256,1024]{1,0:T(8,128)(2,1)} %bitcast.4, s32[2]{0:T(128)} %owner_of.1, s32[2]{0:T(128)} %slot_of.1, ...), custom_call_target="tpu_custom_call" | custom-call | tf_op jit(solution)/shard_map/pallas_call | solution.py:519
  59.5 1.2 %copy.13 = bf16[8,32]{1,0:T(8,128)(2,1)} copy(bf16[8,32]{1,0:T(8,128)(2,1)} %get-tuple-element.4) | data formatting | bytes 1024
  60.7 1.3 %copy.14 = f32[8,32]{1,0:T(8,128)} copy(f32[8,32]{1,0:T(8,128)} %get-tuple-element.5) | data formatting | bytes 2048

commit v2 on v1

v2 whole, which is shorter than its diff:
```python
import functools

import jax
import jax.numpy as jnp
from jax import lax
from jax.experimental import pallas as pl
from jax.experimental.pallas import tpu as pltpu
from jax.sharding import Mesh
from jax.sharding import PartitionSpec as P

AXES = ("vir_0", "vir_1", "vir_2", "ph", "vec")
VIR = ("vir_0", "vir_1", "vir_2")
VIR_PH = ("vir_0", "vir_1", "vir_2", "ph")
F32 = jnp.float32
BF16 = jnp.bfloat16
R = 8
LANES = 128


def far_first(count):
    return sorted(range(1, count), key=lambda d: -min(d, count - d))


def slot_at(delta, count):
    return jnp.where(delta * 2 <= count, jnp.maximum(2 * delta - 1, 0), 2 * (count - delta))


def slot_order(count):
    order = [0]
    for d in range(1, count // 2 + 1):
        order += [d, count - d] if 2 * d < count else [d]
    return order


def body(
    sizes,
    factor,
    amp,
    cycle_amp,
    ov_slots,
    owner_of,
    slot_of,
    ov_pairs,
    eps_vir,
    eps_occ,
    out_ref,
    out_v,
    owner_s,
    slot_s,
    eps_vir_s,
    eps_occ_s,
    factor_raw,
    factor_wide,
    factor_t,
    amp_raw,
    amp_wide,
    amp_d,
    rows,
    row_lhs,
    half_sum,
    half,
    slots_v,
    cyc_v,
    pairs_v,
    blk_send,
    blk_recv,
    part,
    part_recv,
    c1,
    c1_recv,
    c2,
    c2_recv,
    cyc,
    cyc_recv,
    grid,
    grid_recv,
    wide,
    stage,
    stage_recv,
    second,
    second_recv,
    third,
    third_recv,
    tally,
    load_sem,
    send_sem,
    recv_sem,
):
    nx, nl, ny, nh, nk = sizes
    pc = factor.shape[0]
    pairs = amp.shape[2]
    slab = nl * ny * R
    part_rows = ny * R
    x, l, y, h, k = (lax.axis_index(a) for a in AXES)
    me = {"vir_0": x, "vir_1": l, "vir_2": y, "ph": h, "vec": k}

    def at(**moved):
        return tuple(moved.get(a, me[a]) for a in AXES)

    def step(axis, value, d, count):
        return {axis: lax.rem(value + d, count)}

    ids = iter(range(1000))

    def remote(src, dst, target, slot):
        return pltpu.make_async_remote_copy(
            src_ref=src,
            dst_ref=dst,
            send_sem=send_sem.at[0],
            recv_sem=recv_sem.at[slot],
            device_id=target,
            device_id_type=pl.DeviceIdType.MESH,
        )

    unit = R * pc * 2
    sent_units = []

    def exchange(copies):
        slot = next(ids)
        units = 0
        for src, dst, moved in copies:
            remote(src, dst, at(**moved), slot).start()
            units += src.size * src.dtype.itemsize // unit
        sent_units.append(units)
        whole = tally.at[pl.ds(0, units)]
        return remote(whole, whole, at(**copies[0][2]), slot)

    x_steps, y_steps = far_first(nx), far_first(ny)

    z_steps = [
        (dl, dh, dk)
        for dh in sorted(range(nh), key=lambda d: -min(d, nh - d))
        for dl in range(nl)
        for dk in range(nk)
        if dl or dh or dk
    ]
    z_partners = [
        {**step("vir_1", l, dl, nl), **step("ph", h, dh, nh), **step("vec", k, dk, nk)}
        for dl, dh, dk in z_steps
    ]

    loads = []

    def load(whole, *copies):
        sem = load_sem.at[len(loads)]
        for src, dst in copies:
            pltpu.make_async_copy(src, dst, sem).start()
        loads.append(pltpu.make_async_copy(whole, whole, sem))
        return loads[-1]

    def slab_copy(s):
        return factor.at[:, :, pl.ds(s * slab, slab)], factor_raw.at[s]

    first_load = load(factor_raw.at[0], slab_copy(0))
    block_loads = [
        load(owner_s, (owner_of, owner_s)),
        load(slot_s, (slot_of, slot_s)),
        load(cyc_v, (cycle_amp, cyc_v)),
    ]

    barrier = pltpu.get_barrier_semaphore()
    partners = []
    for dx, dy in zip(x_steps, y_steps):
        for dl in reversed(range(nl)):
            partners.append({**step("vir_0", x, dx, nx), **step("vir_1", l, dl, nl)})
            partners.append({**step("vir_2", y, dy, ny), **step("vir_1", l, dl, nl)})
    for moved in partners + z_partners:
        pl.semaphore_signal(
            barrier, inc=1, device_id=at(**moved), device_id_type=pl.DeviceIdType.MESH
        )

    slots_load = load(slots_v, (ov_slots, slots_v))
    factor_load = load(factor_raw.at[1:], *[slab_copy(s) for s in range(1, nx)])
    amp_load = load(
        amp_raw,
        *[
            (amp.at[pl.ds(s * slab, slab)], amp_raw.at[pl.ds(s * slab, slab)])
            for s in range(nx)
        ],
    )
    late_loads = [
        load(pairs_v, (ov_pairs, pairs_v)),
        load(eps_vir_s, (eps_vir, eps_vir_s)),
        load(eps_occ_s, (eps_occ, eps_occ_s)),
    ]

    first_load.wait()
    first = factor_raw[0].astype(F32)[:, :, :1]
    lane_of = lax.broadcasted_iota(jnp.int32, (pc, R, pc), 2)
    row_of = lax.broadcasted_iota(jnp.int32, (pc, R, pc), 0)
    piece = jnp.sum(jnp.where(lane_of == row_of, first, 0.0), axis=0).astype(BF16)
    outer = jnp.where(l == 0, y, x)
    inner = jnp.where(l == 0, x, y)
    rows[l, outer, inner] = piece

    for copy in block_loads:
        copy.wait()
    blocks = [jnp.concatenate([cyc_v[n].astype(F32)] * 2, axis=1) for n in range(2)]
    lane_half = (
        lax.broadcasted_iota(jnp.int32, blocks[0].shape, 1) >= blocks[0].shape[1] // 2
    ).astype(jnp.int32)
    for target in range(nh):
        for pair in range(2):
            total = jnp.zeros_like(blocks[0])
            for n in range(2):
                wanted = jnp.where(owner_s[n] == target, slot_s[n], -1)
                total = total + jnp.where(lane_half + 2 * pair == wanted, blocks[n], 0.0)
            blk_send[target, pair] = total.astype(BF16)

    pl.semaphore_wait(barrier, len(partners) + len(z_partners))

    pick = rows.at[l, outer, inner]
    copies = []
    for d in far_first(nx) + [0]:
        for dl in reversed(range(nl)):
            if d or dl:
                moved = {
                    "vir_0": lax.rem(x + d * (1 - l), nx),
                    "vir_2": lax.rem(y + d * l, ny),
                    **step("vir_1", l, dl, nl),
                }
                copies.append((pick, pick, moved))
    gather1 = exchange(copies)
    owners = []
    for d in far_first(nh):
        moved = step("ph", h, d, nh)
        owners.append((blk_send.at[moved["ph"]], blk_recv.at[d - 1], moved))
    to_owner = exchange(owners)

    factor_load.wait()

    def turn_factor(s, carry):
        factor_wide[...] = factor_raw[s].astype(F32).reshape(factor_wide.shape)
        base = pl.multiple_of(s * part_rows, part_rows)
        for d in range(R):
            turned = factor_wide[pl.ds(d, pc, stride=R), :].T.astype(BF16)
            for c in range(nl):
                factor_t[c, pl.ds(base, part_rows), d * pc : (d + 1) * pc] = turned[
                    c * part_rows : (c + 1) * part_rows
                ]
        return carry

    lax.fori_loop(0, nx, turn_factor, 0)

    order_x, order_y = slot_order(nx), slot_order(ny)
    groups = [(0, nx // 2), (nx // 2, nx * 3 // 4), (nx * 3 // 4, nx)] if nx > 2 else [(0, 2)]

    gather1.wait_recv()
    gather2 = []
    for low_slot, high_slot in reversed(groups):
        copies = []
        for dx, dy in zip(x_steps, y_steps):
            own0, own1 = rows.at[0, y], rows.at[1, x]
            if low_slot <= order_y.index(ny - dy) < high_slot:
                copies.append((own0, own0, step("vir_2", y, dy, ny)))
                copies.append((own1, own1, step("vir_0", x, dx, nx)))
        gather2.insert(0, exchange(copies))

    slots_load.wait()
    to_owner.wait_recv()
    arranged = blk_send[h].astype(F32)
    for d in range(nh - 1):
        arranged = arranged + blk_recv[d].astype(F32)
    arranged = arranged.astype(BF16)
    depth = slots_v.shape[0] // 2
    for q in range(nh * nk):
        chunk = slice(q * pc, (q + 1) * pc)
        part[q] = (
            jnp.dot(arranged[0], slots_v[:depth, chunk], preferred_element_type=F32)
            + jnp.dot(arranged[1], slots_v[depth:, chunk], preferred_element_type=F32)
        ).astype(BF16)
    copies = []
    for n, moved in enumerate(z_partners):
        copies.append((part.at[moved["ph"] * nk + moved["vec"]], part_recv.at[n], moved))
    to_chunk = exchange(copies)

    amp_load.wait()

    def split_amp(s, carry):
        for u in range(2):
            chunk = amp_raw[pl.ds(pl.multiple_of((2 * s + u) * slab, slab), slab)].astype(F32)
            for n in range(pairs // LANES):
                amp_wide[u, n] = chunk[:, :, n * LANES : (n + 1) * LANES].reshape(slab * R, LANES)
        for d in range(R):
            for n in range(pairs // LANES):
                columns = slice(n * LANES, (n + 1) * LANES)
                for t in range(ny):
                    both = [amp_wide[u, n, pl.ds(t * R * R + d, R, stride=R), :] for u in range(2)]
                    place = slot_at(lax.rem(t - y + ny, ny), ny)
                    amp_d[d, place, pl.ds(pl.multiple_of(s * 2 * R, 2 * R), 2 * R), columns] = (
                        jnp.concatenate(both, axis=0).astype(BF16)
                    )
                for u in range(2):
                    place = slot_at(lax.rem(2 * s + u - x + nx, nx), nx)
                    amp_d[d, place, part_rows:, columns] = amp_wide[
                        u, n, pl.ds(part_rows * R + d, part_rows, stride=R), :
                    ].astype(BF16)
        return carry

    lax.fori_loop(0, nx // 2, split_amp, 0)

    mid = c1.shape[1]
    for index, (low_slot, high_slot) in enumerate(groups):
        gather2[index].wait_recv()
        for s in range(low_slot, high_slot):
            low = rows[0, lax.rem(y + order_y[s], ny)].astype(F32).reshape(part_rows, pc)
            high = rows[1, lax.rem(x + order_x[s], nx)].astype(F32).reshape(part_rows, pc)
            row_lhs[:, s * slab : (s + 1) * slab] = (
                jnp.concatenate([low, high], axis=0).T.astype(BF16)
            )

        def make_half(d, carry):
            lines = pl.ds(pl.multiple_of(d * pc, pc), pc)
            depth = (high_slot - low_slot) * slab
            value = jnp.dot(
                row_lhs[:, low_slot * slab : high_slot * slab],
                amp_d[d, low_slot:high_slot].reshape(depth, pairs),
                preferred_element_type=F32,
            )
            if index:
                value = half_sum[lines, :] + value
            if index == len(groups) - 1:
                half[lines, :] = value.astype(BF16)
            else:
                half_sum[lines, :] = value
            return carry

        lax.fori_loop(0, R, make_half, 0, unroll=True)

    swap = []
    for c in range(nl):
        full = jnp.dot(factor_t[c], half[...], preferred_element_type=F32)
        for n in range(nk):
            grid[c, n] = full[:, n * LANES : (n + 1) * LANES].reshape(nx, ny, R, LANES)
        swap.append(
            exchange([(grid.at[c, 1 - k], grid_recv.at[c], step("vec", k, 1, nk))])
        )
        if c == 0:
            to_chunk.wait_recv()
            total = part[h * nk + k].astype(F32)
            for n in range(len(z_partners)):
                total = total + part_recv[n].astype(F32)
            c1[0], c1[1] = total[:mid], total[mid:]
            copies = []
            for dx, dy in zip(x_steps, y_steps):
                copies.append((c1.at[0], c1_recv.at[0, dx - 1], step("vir_0", x, dx, nx)))
                copies.append((c1.at[1], c1_recv.at[1, dy - 1], step("vir_2", y, dy, ny)))
            sum1 = exchange(copies)

    scatter1 = []
    for c in range(nl):
        swap[c].wait_recv()
        wide[c] = grid[c, k] + grid_recv[c]
        if c == 0:
            stage[0] = wide[0].astype(BF16)
        else:
            for s in range(nx):
                for t in range(ny):
                    stage[1, t, s] = wide[1, s, t].astype(BF16)
        copies = []
        for d in x_steps if c == 0 else y_steps:
            moved = step("vir_0", x, d, nx) if c == 0 else step("vir_2", y, d, ny)
            there = moved["vir_0"] if c == 0 else moved["vir_2"]
            copies.append((stage.at[c, there], stage_recv.at[c, d - 1], moved))
        scatter1.append(exchange(copies))

    sum1.wait_recv()
    for c in range(2):
        total = c1[c]
        for d in range(nx - 1):
            total = total + c1_recv[c, d]
        c2[c] = total
    copies = []
    for dx, dy in zip(x_steps, y_steps):
        copies.append((c2.at[0], c2_recv.at[0, dy - 1], step("vir_2", y, dy, ny)))
        copies.append((c2.at[1], c2_recv.at[1, dx - 1], step("vir_0", x, dx, nx)))
    sum2 = exchange(copies)

    scatter2 = []
    for c in range(nl):
        scatter1[c].wait_recv()
        total = wide[0, x] if c == 0 else wide[1, :, y]
        for d in range(nx - 1):
            total = total + stage_recv[c, d].astype(F32)
        second[c] = total
        copies = []
        for d in y_steps if c == 0 else x_steps:
            moved = step("vir_2", y, d, ny) if c == 0 else step("vir_0", x, d, nx)
            there = moved["vir_2"] if c == 0 else moved["vir_0"]
            copies.append((second.at[c, there], second_recv.at[c, d - 1], moved))
        scatter2.append(exchange(copies))

    sum2.wait_recv()
    both = []
    for c in range(2):
        total = c2[c]
        for d in range(nx - 1):
            total = total + c2_recv[c, d]
        both.append(total)
    coupling = jnp.concatenate(both, axis=0)
    occ = coupling.shape[0]
    spread = jnp.broadcast_to(coupling[:, None, :], (occ, R, pc)).reshape(occ * R, pc)
    for copy in late_loads:
        copy.wait()
    second_count = ov_pairs.shape[0]
    ov = pairs_v[...].astype(F32).reshape(second_count * R, pc).astype(BF16)
    every = lax.dot_general(
        ov, spread.astype(BF16), (((1,), (1,)), ((), ())), preferred_element_type=F32
    )
    lane_j = lax.rem(lax.broadcasted_iota(jnp.int32, (R, pairs), 1), second_count)
    term = jnp.zeros((R, pairs), F32)
    for j in range(second_count):
        term = term + jnp.where(lane_j == j, every[j * R : (j + 1) * R], 0.0)
    for n in range(nk):
        cyc[n] = term[:, n * LANES : (n + 1) * LANES]
    swap_cyc = exchange([(cyc.at[1 - k], cyc_recv, step("vec", k, 1, nk))])

    width = out_ref.shape[2]
    per_half = LANES // width
    q = h * nk + k
    line = lax.broadcasted_iota(jnp.int32, (R, width), 0)
    lane = lax.broadcasted_iota(jnp.int32, (R, width), 1)
    slab_start = ((x * nl + l) * ny + y) * R
    virtual = jnp.zeros((R, width), F32)
    for r in range(R):
        virtual = jnp.where(line == r, eps_vir_s[slab_start + r], virtual)
    first_occ = jnp.zeros((R, width), F32)
    for n in range(width // second_count):
        first_occ = jnp.where(
            lane // second_count == n, eps_occ_s[q * (width // second_count) + n], first_occ
        )
    second_occ = jnp.zeros((R, width), F32)
    for n in range(second_count):
        second_occ = jnp.where(lax.rem(lane, second_count) == n, eps_occ_s[n], second_occ)
    denominator = (eps_vir_s[0] + virtual) - first_occ - second_occ

    swap_cyc.wait_recv()
    cycle_half = cyc[k] + cyc_recv[...]
    for c in range(nl):
        scatter2[c].wait_recv()
        total = second[0, y] if c == 0 else second[1, x]
        for d in range(nx - 1):
            total = total + second_recv[c, d]
        third[c] = total + jnp.where(l == c, cycle_half, 0.0)

    last = next(ids)
    mine = h * nl + l
    own_source = q // per_half == k
    for m in range(per_half):
        for c in range(nl):
            there = k * per_half + m
            th, tk = there // nk, lax.rem(there, nk)
            away = jnp.logical_not((th == h) & (tk == k) & (c == l))
            copy = pltpu.make_async_remote_copy(
                src_ref=third.at[c],
                dst_ref=third_recv.at[mine],
                send_sem=send_sem.at[1],
                recv_sem=recv_sem.at[last],
                device_id=at(ph=th, vec=tk, vir_1=jnp.int32(c)),
                device_id_type=pl.DeviceIdType.MESH,
            )
            pl.when(away)(copy.start)

    @pl.when(own_source)
    def _():
        third_recv[mine] = third[l]

    def finals(count):
        whole = third_recv.at[pl.ds(0, count)]
        return pltpu.make_async_remote_copy(
            src_ref=whole,
            dst_ref=whole,
            send_sem=send_sem.at[1],
            recv_sem=recv_sem.at[last],
            device_id=at(**step("vir_1", l, 1, nl)),
            device_id_type=pl.DeviceIdType.MESH,
        )

    others = per_half * nl

    whole = tally.at[pl.ds(0, sum(sent_units))]
    remote(whole, whole, at(**step("vec", k, 1, nk)), 0).wait_send()
    pl.when(own_source)(finals(others - 1).wait_recv)
    pl.when(jnp.logical_not(own_source))(finals(others).wait_recv)

    total = third_recv[0]
    for s in range(1, nh * nl):
        total = total + third_recv[s]
    mine_lanes = lax.rem(q, per_half)
    result = jnp.zeros((R, width), F32)
    for m in range(per_half):
        result = jnp.where(mine_lanes == m, total[:, m * width : (m + 1) * width], result)
    out_v[0] = result.astype(BF16).astype(F32)
    out_v[1] = denominator
    final_copy = pltpu.make_async_copy(out_v, out_ref, load_sem.at[0])
    final_copy.start()
    pl.when(own_source)(finals(others - 1).wait_send)
    pl.when(jnp.logical_not(own_source))(finals(others).wait_send)
    final_copy.wait()


def local(
    sizes,
    vv_factor,
    ladder_amp,
    cycle_amp,
    ov_slots,
    owner_of,
    slot_of,
    ov_pairs,
    eps_vir,
    eps_occ,
):
    nx, nl, ny, nh, nk = sizes
    pc, _, virtuals = vv_factor.shape
    pairs = ladder_amp.shape[2]
    capacity, chol, part_w = ov_slots.shape
    occ = cycle_amp.shape[1]
    second_count = ov_pairs.shape[1]
    slots_t = jnp.transpose(ov_slots, (0, 2, 1)).reshape(capacity * part_w, chol)
    pairs_t = jnp.transpose(ov_pairs, (1, 2, 0))
    slab = nl * ny * R
    width = pairs // (nh * nk)
    steps = nx - 1
    VM = pltpu.VMEM
    scratch = [
        VM((2, R, width), F32),
        pltpu.SMEM(owner_of.shape, jnp.int32),
        pltpu.SMEM(slot_of.shape, jnp.int32),
        pltpu.SMEM(eps_vir.shape, F32),
        pltpu.SMEM(eps_occ.shape, F32),
        VM((nx, pc, R, slab), BF16),
        VM((pc * R, slab), F32),
        VM((nl, nx * ny * R, R * pc), BF16),
        VM(ladder_amp.shape, BF16),
        VM((2, pairs // LANES, slab * R, LANES), F32),
        VM((R, nx, slab, pairs), BF16),
        VM((nl, nx, ny, R, pc), BF16),
        VM((pc, virtuals), BF16),
        VM((R * pc, pairs), F32),
        VM((R * pc, pairs), BF16),
        VM(slots_t.shape, BF16),
        VM(cycle_amp.shape, BF16),
        VM(pairs_t.shape, BF16),
        VM((nh, 2, occ, 2 * part_w), BF16),
        VM((nh - 1, 2, occ, 2 * part_w), BF16),
        VM((nh * nk, occ, pc), BF16),
        VM((nh * nk * nl - 1, occ, pc), BF16),
        VM((2, occ // 2, pc), F32),
        VM((2, steps, occ // 2, pc), F32),
        VM((2, occ // 2, pc), F32),
        VM((2, steps, occ // 2, pc), F32),
        VM((nk, R, LANES), F32),
        VM((R, LANES), F32),
        VM((nl, nk, nx, ny, R, LANES), F32),
        VM((nl, nx, ny, R, LANES), F32),
        VM((nl, nx, ny, R, LANES), F32),
        VM((nl, nx, ny, R, LANES), BF16),
        VM((nl, steps, ny, R, LANES), BF16),
        VM((nl, ny, R, LANES), F32),
        VM((nl, steps, R, LANES), F32),
        VM((nl, R, LANES), F32),
        VM((nh * nl, R, LANES), F32),
        VM((1024, R, pc), BF16),
        pltpu.SemaphoreType.DMA((10,)),
        pltpu.SemaphoreType.DMA((2,)),
        pltpu.SemaphoreType.DMA((16,)),
    ]
    hbm = pl.BlockSpec(memory_space=pltpu.MemorySpace.HBM)
    out = pl.pallas_call(
        functools.partial(body, sizes),
        out_shape=jax.ShapeDtypeStruct((2, R, width), F32),
        in_specs=[hbm] * 9,
        out_specs=hbm,
        scratch_shapes=scratch,
        compiler_params=pltpu.CompilerParams(
            collective_id=0, has_side_effects=True, vmem_limit_bytes=63 * 1024 * 1024
        ),
    )(
        vv_factor,
        ladder_amp,
        cycle_amp,
        slots_t,
        owner_of,
        slot_of,
        pairs_t,
        eps_vir,
        eps_occ,
    )
    residual = out[0].astype(BF16)
    return residual, residual.astype(F32) / out[1]


def build(devices, sizes):
    torus = Mesh(devices.reshape(sizes), AXES)
    placed = (
        P(("ph", "vec"), VIR, None),
        P(None, VIR, None),
        P(VIR_PH, None, "vec"),
        P(VIR_PH, None, "vec"),
        P(VIR_PH),
        P(VIR_PH),
        P(("ph", "vec"), None, VIR),
        P(),
        P(),
    )
    return jax.shard_map(
        functools.partial(local, sizes),
        mesh=torus,
        in_specs=placed,
        out_specs=(P(VIR, ("ph", "vec")), P(VIR, ("ph", "vec"))),
        check_vma=False,
    )


def solution(mesh):
    return build(mesh.devices, (8, 2, 8, mesh.shape["ph"], mesh.shape["vec"]))
```

time: 62.2 us -> 54.7 us (0.88)
  Pallas kernels: 58.8 us -> 52.6 us
  local copies, waits for them, and re-layouts: 2.5 us -> 0 us
  other arithmetic: 0 us -> 1.28 us
    pallas_call x1, Pallas kernels: 58.8 us -> 52.6 us  [local(): pl.pallas_call(functools.partial(body, sizes), out_shape=jax.ShapeDtypeSt...]
    unnamed x2 -> x0, local copies, waits for them, and re-layouts: 2.5 us -> none
    div x0 -> x1, other arithmetic: none -> 1.28 us  [local(): return (residual, residual.astype(F32) / out[1])]
where the time goes in v2:
time: 54.7 us; the launch traced here: 54.6 us
  Pallas kernels  52.6 us (96%)
  other arithmetic  1.28 us (2%)
  between operations  0.64 us (1%)
    pallas_call x1, Pallas kernels, local(): pl.pallas_call(functools.partial(body, sizes), out_shape=jax.ShapeDtypeSt...  52.6 us
    div x1, other arithmetic, local(): return (residual, residual.astype(F32) / out[1])  1.28 us

profile of v2, /device:TPU:1, one launch (start us, length us, event | category | flops | bytes accessed | tf_op | source)
XLA Modules:
  0.0 54.6 jit_solution(8645818626589121100)
XLA Ops:
  0.6 52.6 %shard_map.104 = f32[2,8,32]{2,1,0:T(8,128)} custom-call(bf16[128,8,1024]{2,1,0:T(8,128)(2,1)} %factor.1, bf16[1024,8,256]{2,1,0:T(8,128)(2,1)} %amp.1, bf16[2,32,64]{2,1,0:T(8,128)(2,1)} %cycle_amp.1, bf16[256,1024]{1,0:T(8,128)(2,1)} %bitcast.9, s32[2]{0:T(128)} %owner_of.1, s32[2]{0:T(128)} %slot_of.1, bf16[8,8,128]{2,1,0:T(8,128)(2,1)} %bitcast.10, ...), custom_call_target="tpu_custom_call" | custom-call | tf_op jit(solution)/shard_map/pallas_call | solution.py:570
  53.3 1.3 %bitcast_divide_fusion = (f32[8,32]{1,0:T(8,128)}, bf16[8,32]{1,0:T(8,128)(2,1)}) fusion(f32[2,8,32]{2,1,0:T(8,128)} %shard_map.104), kind=kLoop, calls=%fused_computation.1 | loop fusion | flops 512 | bytes 3072 | tf_op jit(solution)/shard_map/div | solution.py:591

commit v3 on v2

--- a/solution.py
+++ b/solution.py
@@ -44,7 +44,6 @@
     eps_vir,
     eps_occ,
     out_ref,
-    out_v,
     owner_s,
     slot_s,
     eps_vir_s,
@@ -138,6 +137,7 @@
         {**step("vir_1", l, dl, nl), **step("ph", h, dh, nh), **step("vec", k, dk, nk)}
         for dl, dh, dk in z_steps
     ]
+    z_hops = [nl * min(dh, nh - dh) + dl for dl, dh, dk in z_steps]
 
     loads = []
 
@@ -159,12 +159,13 @@
     ]
 
     barrier = pltpu.get_barrier_semaphore()
-    partners = []
+    partners = list(zip(z_hops, z_partners))
     for dx, dy in zip(x_steps, y_steps):
         for dl in reversed(range(nl)):
-            partners.append({**step("vir_0", x, dx, nx), **step("vir_1", l, dl, nl)})
-            partners.append({**step("vir_2", y, dy, ny), **step("vir_1", l, dl, nl)})
-    for moved in partners + z_partners:
+            far_x, far_y = min(dx, nx - dx) + dl, min(dy, ny - dy) + dl
+            partners.append((far_x, {**step("vir_0", x, dx, nx), **step("vir_1", l, dl, nl)}))
+            partners.append((far_y, {**step("vir_2", y, dy, ny), **step("vir_1", l, dl, nl)}))
+    for _, moved in sorted(partners, key=lambda partner: -partner[0]):
         pl.semaphore_signal(
             barrier, inc=1, device_id=at(**moved), device_id_type=pl.DeviceIdType.MESH
         )
@@ -207,7 +208,7 @@
                 total = total + jnp.where(lane_half + 2 * pair == wanted, blocks[n], 0.0)
             blk_send[target, pair] = total.astype(BF16)
 
-    pl.semaphore_wait(barrier, len(partners) + len(z_partners))
+    pl.semaphore_wait(barrier, len(partners))
 
     pick = rows.at[l, outer, inner]
     copies = []
@@ -226,53 +227,6 @@
         moved = step("ph", h, d, nh)
         owners.append((blk_send.at[moved["ph"]], blk_recv.at[d - 1], moved))
     to_owner = exchange(owners)
-
-    factor_load.wait()
-
-    def turn_factor(s, carry):
-        factor_wide[...] = factor_raw[s].astype(F32).reshape(factor_wide.shape)
-        base = pl.multiple_of(s * part_rows, part_rows)
-        for d in range(R):
-            turned = factor_wide[pl.ds(d, pc, stride=R), :].T.astype(BF16)
-            for c in range(nl):
-                factor_t[c, pl.ds(base, part_rows), d * pc : (d + 1) * pc] = turned[
-                    c * part_rows : (c + 1) * part_rows
-                ]
-        return carry
-
-    lax.fori_loop(0, nx, turn_factor, 0)
-
-    order_x, order_y = slot_order(nx), slot_order(ny)
-    groups = [(0, nx // 2), (nx // 2, nx * 3 // 4), (nx * 3 // 4, nx)] if nx > 2 else [(0, 2)]
-
-    gather1.wait_recv()
-    gather2 = []
-    for low_slot, high_slot in reversed(groups):
-        copies = []
-        for dx, dy in zip(x_steps, y_steps):
-            own0, own1 = rows.at[0, y], rows.at[1, x]
-            if low_slot <= order_y.index(ny - dy) < high_slot:
-                copies.append((own0, own0, step("vir_2", y, dy, ny)))
-                copies.append((own1, own1, step("vir_0", x, dx, nx)))
-        gather2.insert(0, exchange(copies))
-
-    slots_load.wait()
-    to_owner.wait_recv()
-    arranged = blk_send[h].astype(F32)
-    for d in range(nh - 1):
-        arranged = arranged + blk_recv[d].astype(F32)
-    arranged = arranged.astype(BF16)
-    depth = slots_v.shape[0] // 2
-    for q in range(nh * nk):
-        chunk = slice(q * pc, (q + 1) * pc)
-        part[q] = (
-            jnp.dot(arranged[0], slots_v[:depth, chunk], preferred_element_type=F32)
-            + jnp.dot(arranged[1], slots_v[depth:, chunk], preferred_element_type=F32)
-        ).astype(BF16)
-    copies = []
-    for n, moved in enumerate(z_partners):
-        copies.append((part.at[moved["ph"] * nk + moved["vec"]], part_recv.at[n], moved))
-    to_chunk = exchange(copies)
 
     amp_load.wait()
 
@@ -299,6 +253,53 @@
 
     lax.fori_loop(0, nx // 2, split_amp, 0)
 
+    order_x, order_y = slot_order(nx), slot_order(ny)
+    groups = [(0, nx // 2), (nx // 2, nx * 3 // 4), (nx * 3 // 4, nx)] if nx > 2 else [(0, 2)]
+
+    gather1.wait_recv()
+    gather2 = []
+    for low_slot, high_slot in reversed(groups):
+        copies = []
+        for dx, dy in zip(x_steps, y_steps):
+            own0, own1 = rows.at[0, y], rows.at[1, x]
+            if low_slot <= order_y.index(ny - dy) < high_slot:
+                copies.append((own0, own0, step("vir_2", y, dy, ny)))
+                copies.append((own1, own1, step("vir_0", x, dx, nx)))
+        gather2.insert(0, exchange(copies))
+
+    slots_load.wait()
+    to_owner.wait_recv()
+    arranged = blk_send[h].astype(F32)
+    for d in range(nh - 1):
+        arranged = arranged + blk_recv[d].astype(F32)
+    arranged = arranged.astype(BF16)
+    depth = slots_v.shape[0] // 2
+    for q in range(nh * nk):
+        chunk = slice(q * pc, (q + 1) * pc)
+        part[q] = (
+            jnp.dot(arranged[0], slots_v[:depth, chunk], preferred_element_type=F32)
+            + jnp.dot(arranged[1], slots_v[depth:, chunk], preferred_element_type=F32)
+        ).astype(BF16)
+    copies = []
+    for n, moved in enumerate(z_partners):
+        copies.append((part.at[moved["ph"] * nk + moved["vec"]], part_recv.at[n], moved))
+    to_chunk = exchange(copies)
+
+    factor_load.wait()
+
+    def turn_factor(s, carry):
+        factor_wide[...] = factor_raw[s].astype(F32).reshape(factor_wide.shape)
+        base = pl.multiple_of(s * part_rows, part_rows)
+        for d in range(R):
+            turned = factor_wide[pl.ds(d, pc, stride=R), :].T.astype(BF16)
+            for c in range(nl):
+                factor_t[c, pl.ds(base, part_rows), d * pc : (d + 1) * pc] = turned[
+                    c * part_rows : (c + 1) * part_rows
+                ]
+        return carry
+
+    lax.fori_loop(0, nx, turn_factor, 0)
+
     mid = c1.shape[1]
     for index, (low_slot, high_slot) in enumerate(groups):
         gather2[index].wait_recv()
@@ -335,17 +336,18 @@
         swap.append(
             exchange([(grid.at[c, 1 - k], grid_recv.at[c], step("vec", k, 1, nk))])
         )
-        if c == 0:
-            to_chunk.wait_recv()
-            total = part[h * nk + k].astype(F32)
-            for n in range(len(z_partners)):
-                total = total + part_recv[n].astype(F32)
-            c1[0], c1[1] = total[:mid], total[mid:]
-            copies = []
-            for dx, dy in zip(x_steps, y_steps):
-                copies.append((c1.at[0], c1_recv.at[0, dx - 1], step("vir_0", x, dx, nx)))
-                copies.append((c1.at[1], c1_recv.at[1, dy - 1], step("vir_2", y, dy, ny)))
-            sum1 = exchange(copies)
+
+    to_chunk.wait_recv()
+    total = part[h * nk + k].astype(F32)
+    for n in range(len(z_partners)):
+        total = total + part_recv[n].astype(F32)
+    parts = [total[:mid], total[mid:]]
+    c1[0], c1[1] = [p.astype(BF16) for p in parts]
+    copies = []
+    for dx, dy in zip(x_steps, y_steps):
+        copies.append((c1.at[0], c1_recv.at[0, dx - 1], step("vir_0", x, dx, nx)))
+        copies.append((c1.at[1], c1_recv.at[1, dy - 1], step("vir_2", y, dy, ny)))
+    sum1 = exchange(copies)
 
     scatter1 = []
     for c in range(nl):
@@ -366,10 +368,9 @@
 
     sum1.wait_recv()
     for c in range(2):
-        total = c1[c]
         for d in range(nx - 1):
-            total = total + c1_recv[c, d]
-        c2[c] = total
+            parts[c] = parts[c] + c1_recv[c, d].astype(F32)
+        c2[c] = parts[c].astype(BF16)
     copies = []
     for dx, dy in zip(x_steps, y_steps):
         copies.append((c2.at[0], c2_recv.at[0, dy - 1], step("vir_2", y, dy, ny)))
@@ -393,9 +394,9 @@
     sum2.wait_recv()
     both = []
     for c in range(2):
-        total = c2[c]
+        total = parts[c]
         for d in range(nx - 1):
-            total = total + c2_recv[c, d]
+            total = total + c2_recv[c, d].astype(F32)
         both.append(total)
     coupling = jnp.concatenate(both, axis=0)
     occ = coupling.shape[0]
@@ -413,10 +414,15 @@
         term = term + jnp.where(lane_j == j, every[j * R : (j + 1) * R], 0.0)
     for n in range(nk):
         cyc[n] = term[:, n * LANES : (n + 1) * LANES]
-    swap_cyc = exchange([(cyc.at[1 - k], cyc_recv, step("vec", k, 1, nk))])
+    per_half = LANES // out_ref.shape[2]
+    copies = []
+    for (dl, dh, dk), moved in zip(z_steps, z_partners):
+        if dl == 0:
+            there = moved["ph"] * nk + moved["vec"]
+            copies.append((cyc.at[there // per_half], cyc_recv.at[len(copies)], moved))
+    to_pairs = exchange(copies)
 
     width = out_ref.shape[2]
-    per_half = LANES // width
     q = h * nk + k
     line = lax.broadcasted_iota(jnp.int32, (R, width), 0)
     lane = lax.broadcasted_iota(jnp.int32, (R, width), 1)
@@ -434,14 +440,12 @@
         second_occ = jnp.where(lax.rem(lane, second_count) == n, eps_occ_s[n], second_occ)
     denominator = (eps_vir_s[0] + virtual) - first_occ - second_occ
 
-    swap_cyc.wait_recv()
-    cycle_half = cyc[k] + cyc_recv[...]
     for c in range(nl):
         scatter2[c].wait_recv()
         total = second[0, y] if c == 0 else second[1, x]
         for d in range(nx - 1):
             total = total + second_recv[c, d]
-        third[c] = total + jnp.where(l == c, cycle_half, 0.0)
+        third[c] = total
 
     last = next(ids)
     mine = h * nl + l
@@ -478,25 +482,26 @@
 
     others = per_half * nl
 
+    to_pairs.wait_recv()
+    cycle_sum = cyc[q // per_half]
+    for n in range(nh * nk - 1):
+        cycle_sum = cycle_sum + cyc_recv[n]
     whole = tally.at[pl.ds(0, sum(sent_units))]
     remote(whole, whole, at(**step("vec", k, 1, nk)), 0).wait_send()
     pl.when(own_source)(finals(others - 1).wait_recv)
     pl.when(jnp.logical_not(own_source))(finals(others).wait_recv)
 
-    total = third_recv[0]
-    for s in range(1, nh * nl):
+    total = cycle_sum
+    for s in range(nh * nl):
         total = total + third_recv[s]
     mine_lanes = lax.rem(q, per_half)
     result = jnp.zeros((R, width), F32)
     for m in range(per_half):
         result = jnp.where(mine_lanes == m, total[:, m * width : (m + 1) * width], result)
-    out_v[0] = result.astype(BF16).astype(F32)
-    out_v[1] = denominator
-    final_copy = pltpu.make_async_copy(out_v, out_ref, load_sem.at[0])
-    final_copy.start()
+    out_ref[0] = result.astype(BF16).astype(F32)
+    out_ref[1] = denominator
     pl.when(own_source)(finals(others - 1).wait_send)
     pl.when(jnp.logical_not(own_source))(finals(others).wait_send)
-    final_copy.wait()
 
 
 def local(
@@ -524,7 +529,6 @@
     steps = nx - 1
     VM = pltpu.VMEM
     scratch = [
-        VM((2, R, width), F32),
         pltpu.SMEM(owner_of.shape, jnp.int32),
         pltpu.SMEM(slot_of.shape, jnp.int32),
         pltpu.SMEM(eps_vir.shape, F32),
@@ -546,12 +550,12 @@
         VM((nh - 1, 2, occ, 2 * part_w), BF16),
         VM((nh * nk, occ, pc), BF16),
         VM((nh * nk * nl - 1, occ, pc), BF16),
-        VM((2, occ // 2, pc), F32),
-        VM((2, steps, occ // 2, pc), F32),
-        VM((2, occ // 2, pc), F32),
-        VM((2, steps, occ // 2, pc), F32),
+        VM((2, occ // 2, pc), BF16),
+        VM((2, steps, occ // 2, pc), BF16),
+        VM((2, occ // 2, pc), BF16),
+        VM((2, steps, occ // 2, pc), BF16),
         VM((nk, R, LANES), F32),
-        VM((R, LANES), F32),
+        VM((nh * nk - 1, R, LANES), F32),
         VM((nl, nk, nx, ny, R, LANES), F32),
         VM((nl, nx, ny, R, LANES), F32),
         VM((nl, nx, ny, R, LANES), F32),
@@ -569,9 +573,9 @@
     hbm = pl.BlockSpec(memory_space=pltpu.MemorySpace.HBM)
     out = pl.pallas_call(
         functools.partial(body, sizes),
-        out_shape=jax.ShapeDtypeStruct((2, R, width), F32),
+        out_shape=pltpu.VMEM((2, R, width), F32),
         in_specs=[hbm] * 9,
-        out_specs=hbm,
+        out_specs=pl.BlockSpec(memory_space=pltpu.VMEM),
         scratch_shapes=scratch,
         compiler_params=pltpu.CompilerParams(
             collective_id=0, has_side_effects=True, vmem_limit_bytes=63 * 1024 * 1024

time: 54.7 us -> 52.8 us (0.965)
  Pallas kernels: 52.6 us -> 51.4 us
  other arithmetic: 1.28 us -> 0.6 us
    pallas_call x1, Pallas kernels: 52.6 us -> 51.4 us  [local(): pl.pallas_call(functools.partial(body, sizes), out_shape=pltpu.VMEM((2, R...]
    div x1, other arithmetic: 1.28 us -> 0.6 us  [local(): return (residual, residual.astype(F32) / out[1])]
where the time goes in v3:
time: 52.8 us; the launch traced here: 52.6 us
  Pallas kernels  51.4 us (97%)
  between operations  0.64 us (1%)
  other arithmetic  0.6 us (1%)
    pallas_call x1, Pallas kernels, local(): pl.pallas_call(functools.partial(body, sizes), out_shape=pltpu.VMEM((2, R...  51.4 us

profile of v3, /device:TPU:1, one launch (start us, length us, event | category | flops | bytes accessed | tf_op | source)
XLA Modules:
  0.0 52.6 jit_solution(6173303057150924831)
XLA Ops:
  0.6 51.4 %shard_map.104 = f32[2,8,32]{2,1,0:T(8,128)S(1)} custom-call(bf16[128,8,1024]{2,1,0:T(8,128)(2,1)} %factor.1, bf16[1024,8,256]{2,1,0:T(8,128)(2,1)} %amp.1, bf16[2,32,64]{2,1,0:T(8,128)(2,1)} %cycle_amp.1, bf16[256,1024]{1,0:T(8,128)(2,1)} %bitcast.9, s32[2]{0:T(128)} %owner_of.1, s32[2]{0:T(128)} %slot_of.1, bf16[8,8,128]{2,1,0:T(8,128)(2,1)} %bitcast.10, ...), custom_call_target="tpu_custom_call" | custom-call | tf_op jit(solution)/shard_map/pallas_call | solution.py:574
  52.0 0.6 %bitcast_divide_fusion = (f32[8,32]{1,0:T(8,128)}, bf16[8,32]{1,0:T(8,128)(2,1)}) fusion(f32[2,8,32]{2,1,0:T(8,128)S(1)} %shard_map.104), kind=kLoop, calls=%fused_computation.1 | loop fusion | flops 512 | bytes 3072 | tf_op jit(solution)/shard_map/div | solution.py:595

commit v4 on v3

--- a/solution.py
+++ b/solution.py
@@ -72,6 +72,7 @@
     cyc,
     cyc_recv,
     grid,
+    grid_send,
     grid_recv,
     wide,
     stage,
@@ -333,8 +334,9 @@
         full = jnp.dot(factor_t[c], half[...], preferred_element_type=F32)
         for n in range(nk):
             grid[c, n] = full[:, n * LANES : (n + 1) * LANES].reshape(nx, ny, R, LANES)
+            grid_send[c, n] = grid[c, n].astype(BF16)
         swap.append(
-            exchange([(grid.at[c, 1 - k], grid_recv.at[c], step("vec", k, 1, nk))])
+            exchange([(grid_send.at[c, 1 - k], grid_recv.at[c], step("vec", k, 1, nk))])
         )
 
     to_chunk.wait_recv()
@@ -352,7 +354,7 @@
     scatter1 = []
     for c in range(nl):
         swap[c].wait_recv()
-        wide[c] = grid[c, k] + grid_recv[c]
+        wide[c] = grid[c, k] + grid_recv[c].astype(F32)
         if c == 0:
             stage[0] = wide[0].astype(BF16)
         else:
@@ -557,7 +559,8 @@
         VM((nk, R, LANES), F32),
         VM((nh * nk - 1, R, LANES), F32),
         VM((nl, nk, nx, ny, R, LANES), F32),
-        VM((nl, nx, ny, R, LANES), F32),
+        VM((nl, nk, nx, ny, R, LANES), BF16),
+        VM((nl, nx, ny, R, LANES), BF16),
         VM((nl, nx, ny, R, LANES), F32),
         VM((nl, nx, ny, R, LANES), BF16),
         VM((nl, steps, ny, R, LANES), BF16),

time: 52.8 us -> 53.2 us (level)
  no operation moved by 1% of the time
where the time goes in v4:
time: 53.2 us; the launch traced here: 53 us
  Pallas kernels  51.8 us (97%)
  between operations  0.64 us (1%)
  other arithmetic  0.6 us (1%)
    pallas_call x1, Pallas kernels, local(): pl.pallas_call(functools.partial(body, sizes), out_shape=pltpu.VMEM((2, R...  51.8 us

profile of v4, /device:TPU:1, one launch (start us, length us, event | category | flops | bytes accessed | tf_op | source)
XLA Modules:
  0.0 53.0 jit_solution(16484212848332192521)
XLA Ops:
  0.6 51.8 %shard_map.104 = f32[2,8,32]{2,1,0:T(8,128)S(1)} custom-call(bf16[128,8,1024]{2,1,0:T(8,128)(2,1)} %factor.1, bf16[1024,8,256]{2,1,0:T(8,128)(2,1)} %amp.1, bf16[2,32,64]{2,1,0:T(8,128)(2,1)} %cycle_amp.1, bf16[256,1024]{1,0:T(8,128)(2,1)} %bitcast.9, s32[2]{0:T(128)} %owner_of.1, s32[2]{0:T(128)} %slot_of.1, bf16[8,8,128]{2,1,0:T(8,128)(2,1)} %bitcast.10, ...), custom_call_target="tpu_custom_call" | custom-call | tf_op jit(solution)/shard_map/pallas_call | solution.py:577
  52.4 0.6 %bitcast_divide_fusion = (f32[8,32]{1,0:T(8,128)}, bf16[8,32]{1,0:T(8,128)(2,1)}) fusion(f32[2,8,32]{2,1,0:T(8,128)S(1)} %shard_map.104), kind=kLoop, calls=%fused_computation.1 | loop fusion | flops 512 | bytes 3072 | tf_op jit(solution)/shard_map/div | solution.py:598
